TPU v7x, 32 devices: a whole 2x2x4 slice. The times are simulated.
32 devices in a mesh: mem: 8 (over z, x), head: 4 (over y, core).
Axes of the slice: x: 2, y: 2, z: 4, core: 2. Of those that a mesh axis runs over, the one named last changes fastest.
Arguments:
- tokens: bfloat16 [8192, 4096], P('mem'), may hold values from -14 to 14
- w_query: bfloat16 [4096, 4096], P(None, 'head'), may hold values from -0.09375 to 0.09375
- w_key: bfloat16 [4096, 1024], P(None, 'head'), may hold values from -0.09375 to 0.09375
- w_value: bfloat16 [4096, 1024], P(None, 'head'), may hold values from -0.09375 to 0.09375
- w_out: bfloat16 [4096, 4096], P('head'), may hold values from -0.09375 to 0.09375
- gate_bias: float32 [32], P('head'), may hold values from -4 to 4
- mem_keys: bfloat16 [65536, 1024], P('mem', 'head'), may hold values from -72 to 72
- mem_values: bfloat16 [65536, 1024], P('mem', 'head'), may hold values from -6 to 6
- block_ids: int32 [64, 16], P('mem'), may hold values from 0 to 511, as said below
- block_counts: int32 [512], replicated, may hold values from 1 to 128
Outputs:
- layer_out: bfloat16 [8192, 4096], P('mem', 'head')
Inputs may be any that keep to these rules, and one draw needn't show every extreme that they name: `block_ids`: row c lists 16 different memory blocks; block b lies on index b // 64 of mem. Over the 8 query blocks of one index of mem, every listed block appears in exactly two rows, at most 16 different listed blocks lie on any one index of mem, and in every draw some index of mem has exactly 16 different blocks listed by every index of mem.
All inputs are finite; a program needn't handle non-finite values.
Results may differ from a plain program's by a relative error of at most 0.015.
The roundings to bfloat16 on the way count: a program that leaves them out, or rounds other values in their place, can miss the bound.
Values may be sent and summed in bfloat16 or wider, within the bound.
A program may use at most 320 MiB of HBM per device.

v0:
```python
import jax
import jax.numpy as jnp
from jax import lax
from jax.sharding import PartitionSpec as P

HD = 128
BLK = 128


def attend(queries, key_rows, value_rows, allowed):
    scores = jnp.einsum(
        "qkgd,skd->kgqs", queries, key_rows, preferred_element_type=jnp.float32
    ) * HD ** (-0.5)
    scores = jnp.where(allowed, scores, -jnp.inf)
    peak_score = jnp.max(scores, axis=-1, keepdims=True)
    weights = jnp.exp(scores - peak_score)
    weights = (weights / jnp.sum(weights, axis=-1, keepdims=True)).astype(jnp.bfloat16)
    return jnp.einsum("kgqs,skd->qkgd", weights, value_rows, preferred_element_type=jnp.float32)


def plan_requests(flat_chosen, blocks_each):
    owner_of = flat_chosen // blocks_each
    local_of = flat_chosen % blocks_each
    order = jnp.arange(flat_chosen.shape[0])
    earlier = order[None, :] < order[:, None]
    first_seen = jnp.ones(flat_chosen.shape, jnp.bool_)
    same_owner = owner_of[:, None] == owner_of[None, :]
    first_rank = jnp.sum((same_owner & earlier & first_seen[None, :]).astype(jnp.int32), axis=1)
    return (owner_of, local_of, first_rank, first_seen)


def on_device(
    tokens, w_query, w_key, w_value, w_out, gate_bias, mem_keys, mem_values, block_ids, block_counts
):
    tok_rows = tokens.shape[0]
    qblk_count = tok_rows // BLK
    topk_count = block_ids.shape[1]
    kv_local = w_key.shape[1] // HD
    heads_local = w_query.shape[1] // HD
    per_kv = heads_local // kv_local
    owners = lax.axis_size("mem")
    blocks_each = mem_keys.shape[0] // BLK
    me_index = lax.axis_index("mem")
    block_cap = max(2, topk_count * qblk_count // owners)
    capacity = 2 * block_cap
    all_chosen = lax.all_gather(block_ids, "mem", axis=0, tiled=True).reshape(
        owners, qblk_count * topk_count
    )

    def send_list(flat_chosen):
        owner_of, local_of, rank_of, first_seen = plan_requests(flat_chosen, blocks_each)
        wanted = (owner_of == me_index) & first_seen
        select = wanted[None, :] & (rank_of[None, :] == jnp.arange(capacity)[:, None])
        return jnp.sum(select.astype(jnp.int32) * local_of[None, :], axis=1)

    send_slots = jax.vmap(send_list)(all_chosen)
    key_blocks = mem_keys.reshape(blocks_each, BLK, kv_local * HD)
    value_blocks = mem_values.reshape(blocks_each, BLK, kv_local * HD)
    send_keys = key_blocks[send_slots]
    send_values = value_blocks[send_slots]
    got_keys, got_values = (
        lax.all_to_all(send_keys, "mem", split_axis=0, concat_axis=0, tiled=True),
        lax.all_to_all(send_values, "mem", split_axis=0, concat_axis=0, tiled=True),
    )
    queries = jnp.dot(tokens, w_query, preferred_element_type=jnp.float32).astype(jnp.bfloat16)
    local_keys = jnp.dot(tokens, w_key, preferred_element_type=jnp.float32).astype(jnp.bfloat16)
    local_values = jnp.dot(tokens, w_value, preferred_element_type=jnp.float32).astype(jnp.bfloat16)
    causal = jnp.arange(tok_rows)[None, :] <= jnp.arange(tok_rows)[:, None]
    local_out = attend(
        queries.reshape(tok_rows, kv_local, per_kv, HD),
        local_keys.reshape(tok_rows, kv_local, HD),
        local_values.reshape(tok_rows, kv_local, HD),
        causal[None, None],
    )
    own_flat = block_ids.reshape(-1)
    owner_of, local_of, rank_of, first_seen = plan_requests(own_flat, blocks_each)
    slot_of = owner_of * capacity + rank_of
    key_rows = got_keys.reshape(owners * capacity, BLK, kv_local * HD)[slot_of]
    value_rows = got_values.reshape(owners * capacity, BLK, kv_local * HD)[slot_of]
    key_rows = key_rows.reshape(qblk_count, topk_count * BLK, kv_local, HD)
    value_rows = value_rows.reshape(qblk_count, topk_count * BLK, kv_local, HD)
    total_blocks = block_counts.shape[0]
    filled = jnp.sum(
        jnp.where(own_flat[:, None] == jnp.arange(total_blocks)[None, :], block_counts[None, :], 0),
        axis=1,
    )
    allowed_mem = (jnp.arange(BLK)[None, :] < filled[:, None]).reshape(qblk_count, topk_count * BLK)

    def memory_block(inputs):
        q_blk, k_blk, v_blk, allow_blk = inputs
        return attend(q_blk, k_blk, v_blk, allow_blk[None, None, None, :])

    mem_out = lax.map(
        memory_block,
        (queries.reshape(qblk_count, BLK, kv_local, per_kv, HD), key_rows, value_rows, allowed_mem),
    )
    mem_out = mem_out.reshape(tok_rows, kv_local, per_kv, HD)
    gate = jax.nn.sigmoid(gate_bias).reshape(kv_local, per_kv)[None, :, :, None]
    attn = (
        (gate * mem_out + (1.0 - gate) * local_out)
        .astype(jnp.bfloat16)
        .reshape(tok_rows, heads_local * HD)
    )
    terms = jnp.dot(attn, w_out, preferred_element_type=jnp.float32)
    return lax.psum_scatter(terms.astype(jnp.bfloat16), "head", scatter_dimension=1, tiled=True)


def solution(mesh):
    in_specs = (
        P("mem", None),
        P(None, "head"),
        P(None, "head"),
        P(None, "head"),
        P("head", None),
        P("head"),
        P("mem", "head"),
        P("mem", "head"),
        P("mem", None),
        P(),
    )
    out_specs = P("mem", "head")
    return jax.shard_map(
        on_device, mesh=mesh, in_specs=in_specs, out_specs=out_specs, check_vma=False
    )
```

profile of v0, /device:TPU:0, one launch (start us, length us, event | category | flops | bytes accessed | tf_op | source)
XLA Modules:
  0.0 1164.9 jit_solution(14783743435537035418)
XLA Ops:
  6.6 32.5 %all_gather.3 = s32[64,16]{1,0:T(8,128)S(1)} all-gather(s32[8,16]{1,0:T(8,128)} %param.20), channel_id=1, replica_groups=mesh['mem'=8,'head'=4] {'mem'}, dimensions={0}, use_global_device_ids=true | all-gather | bytes 4608 | tf_op jit(solution)/shard_map/all_gather | solution.py:46
  39.8 11.5 gather_fusion
  51.3 5.9 all-to-all-start
  57.2 11.6 gather_fusion.2
  68.8 345.0 %all-to-all-done = bf16[8,32,128,256]{3,2,1,0:T(8,128)(2,1)} async-done(((bf16[8,32,128,256]{3,2,1,0:T(8,128)(2,1)}), bf16[8,32,128,256]{3,2,1,0:T(8,128)(2,1)}, u32[]{:S(2)}, u32[]{:S(2)}) %all-to-all-start) | async-done | bytes 16777248 | tf_op jit(solution)/shard_map/all_to_all | solution.py:63
  413.8 5.9 all-to-all-start.1
  420.4 13.8 %convolution_convert_fusion.1 = bf16[1024,1024]{0,1:T(8,128)(2,1)S(1)} fusion(bf16[1024,4096]{1,0:T(8,128)(2,1)} %param.12, bf16[4096,1024]{1,0:T(8,128)(2,1)} %param.13), kind=kOutput, calls=%fused_computation.40 | convolution fusion | flops 8590983168 | bytes 18874368 | tf_op jit(solution)/shard_map/dot_general | solution.py:65
  434.2 1.3 copy-done.2
  435.5 1.9 copy.67
  437.5 4.3 copy.44
  443.5 6.7 convolution_convert_fusion.2
  450.2 6.7 convolution_convert_fusion.3
  457.0 18.8 %fusion.32 = (f32[2,4,1024]{2,1,0:T(4,128)S(1)}, f32[2,4,1024,1024]{2,3,1,0:T(8,128)}) fusion(pred[1024,1024]{0,1:T(8,128)(4,1)S(1)} %iota_compare_fusion, bf16[1024,2,128,1]{0,2,3,1:T(8,128)(2,1)} %bitcast.120, bf16[1024,2,4,128]{0,3,2,1:T(8,128)(2,1)S(1)} %bitcast.117), kind=kOutput, calls=%fused_computation.81 | convolution fusion | flops 2181039104 | bytes 37257216 | tf_op jit(solution)/shard_map/sub | solution.py:16
  475.8 12.3 %gather_fusion.1 = bf16[128,128,256]{2,1,0:T(8,128)(2,1)} fusion(bf16[256,128,256]{2,1,0:T(8,128)(2,1)} %bitcast.13, s32[1024]{0:T(1024)S(1)} %pad_clamp_fusion), kind=kCustom, calls=%fused_computation.1 | custom fusion | bytes 16777728 | tf_op jit(solution)/shard_map/gather | solution.py:79
  488.1 12.5 %reshape.370 = bf16[8,2048,2,128]{3,2,1,0:T(2,128)(2,1)} reshape(bf16[128,128,256]{2,1,0:T(8,128)(2,1)} %gather_fusion.1) | data formatting | bytes 16777216 | tf_op jit(solution)/shard_map/reshape | solution.py:81
  500.6 280.1 %all-to-all-done.1 = bf16[8,32,128,256]{3,2,1,0:T(8,128)(2,1)} async-done(((bf16[8,32,128,256]{3,2,1,0:T(8,128)(2,1)}), bf16[8,32,128,256]{3,2,1,0:T(8,128)(2,1)}, u32[]{:S(2)}, u32[]{:S(2)}) %all-to-all-start.1) | async-done | bytes 16777248 | tf_op jit(solution)/shard_map/all_to_all | solution.py:62
  780.7 12.3 %gather_fusion.3 = bf16[128,128,256]{2,1,0:T(8,128)(2,1)} fusion(bf16[256,128,256]{2,1,0:T(8,128)(2,1)} %bitcast.20, s32[1024]{0:T(1024)S(1)} %pad_clamp_fusion), kind=kCustom, calls=%fused_computation.3 | custom fusion | bytes 16777728 | tf_op jit(solution)/shard_map/gather | solution.py:78
  793.0 12.5 %reshape.371 = bf16[8,2048,2,128]{3,2,1,0:T(2,128)(2,1)} reshape(bf16[128,128,256]{2,1,0:T(8,128)(2,1)} %gather_fusion.3) | data formatting | bytes 16777216 | tf_op jit(solution)/shard_map/reshape | solution.py:80
  805.5 247.0 %while.10 = (s32[]{:T(128)}, f32[8,128,2,4,128]{1,0,4,3,2:T(8,128)}, bf16[8,2048,2,128]{3,2,1,0:T(2,128)(2,1)}, pred[8,2048]{1,0:T(8,128)(4,1)S(1)}, bf16[8,2048...) while((s32[]{:T(128)}, f32[8,128,2,4,128]{1,0,4,3,2:T(8,128)}, ...), condition=%wide.region_7.8_spmd, body=%wide.region_4.7_spmd.sunk | while | flops 1090521088 | bytes 43792992 | solution.py:93
  805.7 2.7 constant_dynamic-slice_fusion.3
  808.4 2.2 fusion.53
  810.7 5.9 fusion.54
  816.6 0.8 copy.73
  817.4 4.1 fusion.55
  821.5 15.1 %dynamic_update_slice.5 = f32[8,128,2,4,128]{1,0,4,3,2:T(8,128)} dynamic-update-slice(f32[8,128,2,4,128]{1,0,4,3,2:T(8,128)} %get-tuple-element.136, f32[1,128,2,4,128]{1,0,4,3,2:T(1,128)S(1)} %bitcast.114, s32[]{:T(128)} %get-tuple-element.135, s32[]{:T(128)} %constant.69.clone.1..sunk, s32[]{:T(128)} %constant.69.clone.1..sunk, s32[]{:T(128)} %constant.69.clone.1..sunk, s32[]{:T(128)} %constant.69.clone.1..sunk) | dynamic-update-slice | bytes 1048580 | tf_op jit(solution)/shard_map/while/body/jit(dynamic_update_index_in_dim)/dynamic_update_slice | solution.py:93
  836.6 2.7 constant_dynamic-slice_fusion.3
  839.3 2.2 fusion.53
  841.5 5.9 fusion.54
  848.2 4.1 fusion.55
  852.3 15.1 %dynamic_update_slice.5 = f32[8,128,2,4,128]{1,0,4,3,2:T(8,128)} dynamic-update-slice(f32[8,128,2,4,128]{1,0,4,3,2:T(8,128)} %get-tuple-element.136, f32[1,128,2,4,128]{1,0,4,3,2:T(1,128)S(1)} %bitcast.114, s32[]{:T(128)} %get-tuple-element.135, s32[]{:T(128)} %constant.69.clone.1..sunk, s32[]{:T(128)} %constant.69.clone.1..sunk, s32[]{:T(128)} %constant.69.clone.1..sunk, s32[]{:T(128)} %constant.69.clone.1..sunk) | dynamic-update-slice | bytes 1048580 | tf_op jit(solution)/shard_map/while/body/jit(dynamic_update_index_in_dim)/dynamic_update_slice | solution.py:93
  867.4 2.7 constant_dynamic-slice_fusion.3
  870.1 2.2 fusion.53
  872.4 5.9 fusion.54
  879.1 4.1 fusion.55
  883.2 15.1 %dynamic_update_slice.5 = f32[8,128,2,4,128]{1,0,4,3,2:T(8,128)} dynamic-update-slice(f32[8,128,2,4,128]{1,0,4,3,2:T(8,128)} %get-tuple-element.136, f32[1,128,2,4,128]{1,0,4,3,2:T(1,128)S(1)} %bitcast.114, s32[]{:T(128)} %get-tuple-element.135, s32[]{:T(128)} %constant.69.clone.1..sunk, s32[]{:T(128)} %constant.69.clone.1..sunk, s32[]{:T(128)} %constant.69.clone.1..sunk, s32[]{:T(128)} %constant.69.clone.1..sunk) | dynamic-update-slice | bytes 1048580 | tf_op jit(solution)/shard_map/while/body/jit(dynamic_update_index_in_dim)/dynamic_update_slice | solution.py:93
  898.3 2.7 constant_dynamic-slice_fusion.3
  901.0 2.2 fusion.53
  903.2 5.9 fusion.54
  909.9 4.1 fusion.55
  914.0 15.1 %dynamic_update_slice.5 = f32[8,128,2,4,128]{1,0,4,3,2:T(8,128)} dynamic-update-slice(f32[8,128,2,4,128]{1,0,4,3,2:T(8,128)} %get-tuple-element.136, f32[1,128,2,4,128]{1,0,4,3,2:T(1,128)S(1)} %bitcast.114, s32[]{:T(128)} %get-tuple-element.135, s32[]{:T(128)} %constant.69.clone.1..sunk, s32[]{:T(128)} %constant.69.clone.1..sunk, s32[]{:T(128)} %constant.69.clone.1..sunk, s32[]{:T(128)} %constant.69.clone.1..sunk) | dynamic-update-slice | bytes 1048580 | tf_op jit(solution)/shard_map/while/body/jit(dynamic_update_index_in_dim)/dynamic_update_slice | solution.py:93
  929.1 2.7 constant_dynamic-slice_fusion.3
  931.8 2.2 fusion.53
  934.1 5.9 fusion.54
  940.7 4.1 fusion.55
  944.9 15.1 %dynamic_update_slice.5 = f32[8,128,2,4,128]{1,0,4,3,2:T(8,128)} dynamic-update-slice(f32[8,128,2,4,128]{1,0,4,3,2:T(8,128)} %get-tuple-element.136, f32[1,128,2,4,128]{1,0,4,3,2:T(1,128)S(1)} %bitcast.114, s32[]{:T(128)} %get-tuple-element.135, s32[]{:T(128)} %constant.69.clone.1..sunk, s32[]{:T(128)} %constant.69.clone.1..sunk, s32[]{:T(128)} %constant.69.clone.1..sunk, s32[]{:T(128)} %constant.69.clone.1..sunk) | dynamic-update-slice | bytes 1048580 | tf_op jit(solution)/shard_map/while/body/jit(dynamic_update_index_in_dim)/dynamic_update_slice | solution.py:93
  960.0 2.7 constant_dynamic-slice_fusion.3
  962.7 2.2 fusion.53
  964.9 5.9 fusion.54
  971.6 4.1 fusion.55
  975.7 15.1 %dynamic_update_slice.5 = f32[8,128,2,4,128]{1,0,4,3,2:T(8,128)} dynamic-update-slice(f32[8,128,2,4,128]{1,0,4,3,2:T(8,128)} %get-tuple-element.136, f32[1,128,2,4,128]{1,0,4,3,2:T(1,128)S(1)} %bitcast.114, s32[]{:T(128)} %get-tuple-element.135, s32[]{:T(128)} %constant.69.clone.1..sunk, s32[]{:T(128)} %constant.69.clone.1..sunk, s32[]{:T(128)} %constant.69.clone.1..sunk, s32[]{:T(128)} %constant.69.clone.1..sunk) | dynamic-update-slice | bytes 1048580 | tf_op jit(solution)/shard_map/while/body/jit(dynamic_update_index_in_dim)/dynamic_update_slice | solution.py:93
  990.8 2.7 constant_dynamic-slice_fusion.3
  993.5 2.2 fusion.53
  995.8 5.9 fusion.54
  1002.4 4.1 fusion.55
  1006.5 15.1 %dynamic_update_slice.5 = f32[8,128,2,4,128]{1,0,4,3,2:T(8,128)} dynamic-update-slice(f32[8,128,2,4,128]{1,0,4,3,2:T(8,128)} %get-tuple-element.136, f32[1,128,2,4,128]{1,0,4,3,2:T(1,128)S(1)} %bitcast.114, s32[]{:T(128)} %get-tuple-element.135, s32[]{:T(128)} %constant.69.clone.1..sunk, s32[]{:T(128)} %constant.69.clone.1..sunk, s32[]{:T(128)} %constant.69.clone.1..sunk, s32[]{:T(128)} %constant.69.clone.1..sunk) | dynamic-update-slice | bytes 1048580 | tf_op jit(solution)/shard_map/while/body/jit(dynamic_update_index_in_dim)/dynamic_update_slice | solution.py:93
  1021.7 2.7 constant_dynamic-slice_fusion.3
  1024.4 2.2 fusion.53
  1026.6 5.9 fusion.54
  1033.3 4.1 fusion.55
  1037.4 15.1 %dynamic_update_slice.5 = f32[8,128,2,4,128]{1,0,4,3,2:T(8,128)} dynamic-update-slice(f32[8,128,2,4,128]{1,0,4,3,2:T(8,128)} %get-tuple-element.136, f32[1,128,2,4,128]{1,0,4,3,2:T(1,128)S(1)} %bitcast.114, s32[]{:T(128)} %get-tuple-element.135, s32[]{:T(128)} %constant.69.clone.1..sunk, s32[]{:T(128)} %constant.69.clone.1..sunk, s32[]{:T(128)} %constant.69.clone.1..sunk, s32[]{:T(128)} %constant.69.clone.1..sunk) | dynamic-update-slice | bytes 1048580 | tf_op jit(solution)/shard_map/while/body/jit(dynamic_update_index_in_dim)/dynamic_update_slice | solution.py:93
  1052.5 5.0 reshape.327
  1057.5 13.3 %fusion.22 = bf16[1024,2,4,128]{0,3,2,1:T(8,128)(2,1)S(1)} fusion(f32[1024,2,4,128]{0,3,2,1:T(8,128)} %reshape.327, bf16[1024,2,128,1]{0,2,3,1:T(8,128)(2,1)S(1)} %bitcast.119, f32[2,4,1024,1024]{2,3,1,0:T(8,128)} %get-tuple-element.81, f32[2,4,1024]{2,1,0:T(4,128)S(1)} %get-tuple-element.80, f32[2,4]{1,0:T(2,128)S(1)} %copy-done.8, f32[2,4]{1,0:T(2,128)S(1)} %copy-done.7), kind=kOutput, calls=%fused_computation.37 | convolution fusion | flops 2168455168 | bytes 40403008 | tf_op jit(solution)/shard_map/kgqs,skd->qkgd/dot_general | solution.py:18
  1070.8 15.0 %convolution_convert_fusion = bf16[1024,4096]{1,0:T(8,128)(2,1)} fusion(bf16[1024,1024]{0,1:T(8,128)(2,1)S(1)} %bitcast.118, bf16[1024,4096]{1,0:T(8,128)(2,1)} %param.16), kind=kOutput, calls=%fused_computation.35 | convolution fusion | flops 8594128896 | bytes 18874368 | tf_op jit(solution)/shard_map/dot_general | solution.py:104
  1085.9 71.9 %reduce-scatter.2.cloned.1.call-done = bf16[1024,1024]{1,0:T(8,128)(2,1)} async-done(((bf16[1024,4096]{1,0:T(8,128)(2,1)}), bf16[1024,1024]{1,0:T(8,128)(2,1)}) %reduce-scatter.2.cloned.1.call-update) | async-done | bytes 2097168 | tf_op jit(solution)/shard_map/reduce_scatter | solution.py:105
  (65 shorter events, 9.1 us)
Async XLA Ops:
  6.5 437.0 %copy-start = (bf16[4096,256]{1,0:T(8,128)(2,1)S(1)}, bf16[4096,256]{1,0:T(8,128)(2,1)}, u32[]{:S(2)}) copy-start(bf16[4096,256]{1,0:T(8,128)(2,1)} %param.14) | copy-start | bytes 6291460
  51.3 362.5 %all-to-all-start = ((bf16[8,32,128,256]{3,2,1,0:T(8,128)(2,1)}), bf16[8,32,128,256]{3,2,1,0:T(8,128)(2,1)}, u32[]{:S(2)}, u32[]{:S(2)}) async-start(bf16[8,32,128,256]{3,2,1,0:T(8,128)(2,1)} %bitcast.111), calls=%async_computation | async-start | bytes 33554432 | tf_op jit(solution)/shard_map/all_to_all | solution.py:63
  413.8 6.4 copy-start.4
  413.8 366.9 %all-to-all-start.1 = ((bf16[8,32,128,256]{3,2,1,0:T(8,128)(2,1)}), bf16[8,32,128,256]{3,2,1,0:T(8,128)(2,1)}, u32[]{:S(2)}, u32[]{:S(2)}) async-start(bf16[8,32,128,256]{3,2,1,0:T(8,128)(2,1)} %bitcast.110), calls=%async_computation.1 | async-start | bytes 33554432 | tf_op jit(solution)/shard_map/all_to_all | solution.py:62
  419.7 738.1 %reduce-scatter.2.cloned.1.call-start = ((), (), s32[]{:S(2)}) async-start(), calls=%async_computation.3 | async-start | bytes 10485760 | tf_op jit(solution)/shard_map/reduce_scatter | solution.py:105
  434.2 1.3 copy-start.2
  434.2 7.6 copy-start.5
  434.2 7.9 copy-start.10
  442.2 0.6 copy-start.6
  443.5 6.7 copy-start.9
  450.2 6.7 copy-start.3
  1052.5 5.0 copy-start.7
  1052.5 5.0 copy-start.8
  1052.5 5.0 copy-start.11
  1070.8 86.9 %copy-start.1 = (bf16[4096,256]{1,0:T(8,128)(2,1)S(1)}, bf16[4096,256]{1,0:T(8,128)(2,1)}, u32[]{:S(2)}) copy-start(bf16[4096,256]{1,0:T(8,128)(2,1)} %param.14) | copy-start | bytes 6291460
Sparse Core Ops, SparseCore 0:
  1086.0 71.7 reduce-scatter.1
where the time goes:
time: 1170 us; the launch traced here: 1160 us
  waiting for transfers between devices  697 us (60%)
  local copies, waits for them, and re-layouts  235 us (20%)
  matrix products  125 us (11%)
  other arithmetic  48.9 us (4%)
  blocking collectives  32.5 us (3%)
  between operations  13.9 us (1%)
  starting transfers between devices  12.3 us (1%)
    all_to_all x1, waiting for transfers between devices, on_device(): lax.all_to_all(send_values, 'mem', split_axis=0, concat_axis=0, tiled=True)  345 us
    all_to_all x1, waiting for transfers between devices, on_device(): lax.all_to_all(send_keys, 'mem', split_axis=0, concat_axis=0, tiled=True)  280 us
    dynamic_update_slice x8, local copies, waits for them, and re-layouts, on_device(): lax.map(memory_block, (queries.reshape(qblk_count, BLK, kv_local, per_kv,...  121 us
    reduce_scatter x1, waiting for transfers between devices, on_device(): lax.psum_scatter(terms.astype(jnp.bfloat16), 'head', scatter_dimension=1,...  71.9 us
    sub x8, other arithmetic, attend(): weights = jnp.exp(scores - peak_score)  46.9 us
    dot_general x9, matrix products, attend(): jnp.einsum('kgqs,skd->qkgd', weights, value_rows, preferred_element_type=...  46.1 us
    all_gather x1, blocking collectives, on_device(): lax.all_gather(block_ids, 'mem', axis=0, tiled=True)  32.5 us
    dynamic_slice x24, local copies, waits for them, and re-layouts, on_device(): lax.map(memory_block, (queries.reshape(qblk_count, BLK, kv_local, per_kv,...  28.1 us
  transfers between devices with their start and end apart: 3, of which 3 were waited for; matrix products, arithmetic and copies ran while one was open for 8% of the time, Pallas kernels for 0%

commit v1 on v0

v1 whole, which is shorter than its diff:
```python
import functools

import jax
import jax.numpy as jnp
from jax import lax
from jax.experimental import pallas as pl
from jax.experimental.pallas import tpu as pltpu
from jax.sharding import PartitionSpec as P

HD = 128
BLK = 128
LOG2E = 1.4426950408889634
MIB = 1 << 20


def share_ids_kernel(owners, ids_ref, out_ref, send_sem, recv_sem):
    me = lax.axis_index("mem")
    barrier = pltpu.get_barrier_semaphore()
    for step in range(1, owners):
        peer = lax.rem(me + step, owners)
        pl.semaphore_signal(
            barrier, inc=1, device_id={"mem": peer}, device_id_type=pl.DeviceIdType.MESH
        )
    pl.semaphore_wait(barrier, owners - 1)
    copies = []
    for step in range(1, owners):
        peer = lax.rem(me + step, owners)
        copy = pltpu.make_async_remote_copy(
            src_ref=ids_ref,
            dst_ref=out_ref.at[me],
            send_sem=send_sem.at[step],
            recv_sem=recv_sem.at[step],
            device_id={"mem": peer},
            device_id_type=pl.DeviceIdType.MESH,
        )
        copy.start()
        copies.append(copy)
    out_ref[me] = ids_ref[...]
    for copy in copies:
        copy.wait()


def share_ids(ids, owners):
    return pl.pallas_call(
        functools.partial(share_ids_kernel, owners),
        out_shape=jax.ShapeDtypeStruct((owners,) + ids.shape, ids.dtype),
        in_specs=[pl.BlockSpec(memory_space=pltpu.VMEM)],
        out_specs=pl.BlockSpec(memory_space=pltpu.VMEM),
        scratch_shapes=[
            pltpu.SemaphoreType.DMA((owners,)),
            pltpu.SemaphoreType.DMA((owners,)),
        ],
        compiler_params=pltpu.CompilerParams(collective_id=0, has_side_effects=True),
        name="share_ids",
    )(ids)


def softmax_rows(scores):
    peak = jnp.max(scores, axis=-1, keepdims=True)
    weights = jnp.exp2((scores - peak) * (LOG2E * HD ** -0.5))
    total = jnp.sum(weights, axis=-1, keepdims=True)
    return (weights * (1.0 / total)).astype(jnp.bfloat16)


def local_kernel(per_kv, q_ref, k_ref, v_ref, out_ref):
    start = pl.program_id(1) * BLK
    keys = k_ref[...]
    values = v_ref[...]
    shape = (BLK, keys.shape[0])
    seen = lax.broadcasted_iota(jnp.int32, shape, 1) <= (
        lax.broadcasted_iota(jnp.int32, shape, 0) + start
    )
    for head in range(per_kv):
        cols = slice(head * HD, (head + 1) * HD)
        scores = lax.dot_general(
            q_ref[:, cols], keys, (((1,), (1,)), ((), ())), preferred_element_type=jnp.float32
        )
        weights = softmax_rows(jnp.where(seen, scores, -jnp.inf))
        out_ref[:, cols] = jnp.dot(weights, values, preferred_element_type=jnp.float32)


def local_attention(queries, keys, values, kv_local, per_kv):
    rows = queries.shape[0]
    width = per_kv * HD
    return pl.pallas_call(
        functools.partial(local_kernel, per_kv),
        grid=(kv_local, rows // BLK),
        in_specs=[
            pl.BlockSpec((BLK, width), lambda j, c: (c, j)),
            pl.BlockSpec((rows, HD), lambda j, c: (0, j)),
            pl.BlockSpec((rows, HD), lambda j, c: (0, j)),
        ],
        out_specs=pl.BlockSpec((BLK, width), lambda j, c: (c, j)),
        out_shape=jax.ShapeDtypeStruct(queries.shape, jnp.float32),
        compiler_params=pltpu.CompilerParams(vmem_limit_bytes=40 * MIB),
        cost_estimate=pl.CostEstimate(
            flops=4 * rows * rows * queries.shape[1],
            bytes_accessed=6 * rows * queries.shape[1],
            transcendentals=rows * rows * kv_local * per_kv,
        ),
        name="local_attention",
    )(queries, keys, values)


def weights_kernel(per_kv, topk, slot_ref, q_ref, bias_ref, k_ref, out_ref, picked):
    block = pl.program_id(1)
    for pick in range(topk):
        picked[pick * BLK : (pick + 1) * BLK, :] = k_ref[slot_ref[block * topk + pick]]
    keys = picked[...]
    bias = bias_ref[0]
    for head in range(per_kv):
        scores = lax.dot_general(
            q_ref[:, head * HD : (head + 1) * HD],
            keys,
            (((1,), (1,)), ((), ())),
            preferred_element_type=jnp.float32,
        )
        out_ref[0, 0, head] = softmax_rows(scores + bias)


def memory_weights(slots, queries, bias, keys, kv_local, per_kv, topk):
    rows = queries.shape[0]
    blocks = rows // BLK
    width = topk * BLK
    total = keys.shape[0]
    return pl.pallas_call(
        functools.partial(weights_kernel, per_kv, topk),
        grid_spec=pltpu.PrefetchScalarGridSpec(
            num_scalar_prefetch=1,
            grid=(kv_local, blocks),
            in_specs=[
                pl.BlockSpec((BLK, per_kv * HD), lambda j, c, s: (c, j)),
                pl.BlockSpec((1, 1, width), lambda j, c, s: (c, 0, 0)),
                pl.BlockSpec((total, BLK, HD), lambda j, c, s: (0, 0, j)),
            ],
            out_specs=pl.BlockSpec(
                (1, 1, per_kv, BLK, width), lambda j, c, s: (j, c, 0, 0, 0)
            ),
            scratch_shapes=[pltpu.VMEM((width, HD), jnp.bfloat16)],
        ),
        out_shape=jax.ShapeDtypeStruct((kv_local, blocks, per_kv, BLK, width), jnp.bfloat16),
        compiler_params=pltpu.CompilerParams(vmem_limit_bytes=48 * MIB),
        cost_estimate=pl.CostEstimate(
            flops=2 * rows * width * queries.shape[1],
            bytes_accessed=2 * kv_local * per_kv * rows * width,
            transcendentals=rows * width * kv_local * per_kv,
        ),
        name="memory_weights",
    )(slots, queries, bias, keys)


def mix_kernel(per_kv, topk, slot_ref, w_ref, gate_ref, local_ref, v_ref, out_ref, picked):
    block = pl.program_id(1)
    for pick in range(topk):
        picked[pick * BLK : (pick + 1) * BLK, :] = v_ref[slot_ref[block * topk + pick]]
    values = picked[...]
    for head in range(per_kv):
        cols = slice(head * HD, (head + 1) * HD)
        mem_out = jnp.dot(w_ref[0, 0, head], values, preferred_element_type=jnp.float32)
        gate = gate_ref[:, cols]
        out_ref[:, cols] = (gate * mem_out + (1.0 - gate) * local_ref[:, cols]).astype(
            jnp.bfloat16
        )


def mix_values(slots, weights, gate, local_out, values, kv_local, per_kv, topk):
    rows, cols = local_out.shape
    blocks = rows // BLK
    width = topk * BLK
    total = values.shape[0]
    return pl.pallas_call(
        functools.partial(mix_kernel, per_kv, topk),
        grid_spec=pltpu.PrefetchScalarGridSpec(
            num_scalar_prefetch=1,
            grid=(kv_local, blocks),
            in_specs=[
                pl.BlockSpec((1, 1, per_kv, BLK, width), lambda j, c, s: (j, c, 0, 0, 0)),
                pl.BlockSpec((1, per_kv * HD), lambda j, c, s: (0, j)),
                pl.BlockSpec((BLK, per_kv * HD), lambda j, c, s: (c, j)),
                pl.BlockSpec((total, BLK, HD), lambda j, c, s: (0, 0, j)),
            ],
            out_specs=pl.BlockSpec((BLK, per_kv * HD), lambda j, c, s: (c, j)),
            scratch_shapes=[pltpu.VMEM((width, HD), jnp.bfloat16)],
        ),
        out_shape=jax.ShapeDtypeStruct((rows, cols), jnp.bfloat16),
        compiler_params=pltpu.CompilerParams(vmem_limit_bytes=48 * MIB),
        cost_estimate=pl.CostEstimate(
            flops=2 * rows * width * cols,
            bytes_accessed=2 * kv_local * per_kv * rows * width,
            transcendentals=0,
        ),
        name="mix_values",
    )(slots, weights, gate, local_out, values)


def plan_requests(flat_chosen, blocks_each):
    owner_of = flat_chosen // blocks_each
    local_of = flat_chosen % blocks_each
    order = jnp.arange(flat_chosen.shape[0])
    repeated = (flat_chosen[:, None] == flat_chosen[None, :]) & (order[None, :] < order[:, None])
    first_seen = jnp.logical_not(jnp.any(repeated, axis=1))
    below = (owner_of[:, None] == owner_of[None, :]) & (flat_chosen[None, :] < flat_chosen[:, None])
    rank_of = jnp.sum((below & first_seen[None, :]).astype(jnp.int32), axis=1)
    return (owner_of, local_of, rank_of, first_seen)


def on_device(
    tokens, w_query, w_key, w_value, w_out, gate_bias, mem_keys, mem_values, block_ids, block_counts
):
    tok_rows = tokens.shape[0]
    qblk_count = tok_rows // BLK
    topk_count = block_ids.shape[1]
    kv_local = w_key.shape[1] // HD
    heads_local = w_query.shape[1] // HD
    per_kv = heads_local // kv_local
    owners = lax.axis_size("mem")
    blocks_each = mem_keys.shape[0] // BLK
    me_index = lax.axis_index("mem")
    capacity = max(2, topk_count * qblk_count // owners)
    all_chosen = share_ids(block_ids, owners).reshape(owners, qblk_count * topk_count)

    def send_list(flat_chosen):
        owner_of, local_of, rank_of, first_seen = plan_requests(flat_chosen, blocks_each)
        wanted = (owner_of == me_index) & first_seen
        select = wanted[None, :] & (rank_of[None, :] == jnp.arange(capacity)[:, None])
        return jnp.sum(select.astype(jnp.int32) * local_of[None, :], axis=1)

    send_slots = jax.vmap(send_list)(all_chosen)
    key_blocks = mem_keys.reshape(blocks_each, BLK, kv_local * HD)
    value_blocks = mem_values.reshape(blocks_each, BLK, kv_local * HD)
    got_keys = lax.all_to_all(
        key_blocks[send_slots], "mem", split_axis=0, concat_axis=0, tiled=True
    ).reshape(owners * capacity, BLK, kv_local * HD)
    got_values = lax.all_to_all(
        value_blocks[send_slots], "mem", split_axis=0, concat_axis=0, tiled=True
    ).reshape(owners * capacity, BLK, kv_local * HD)
    queries = jnp.dot(tokens, w_query, preferred_element_type=jnp.float32).astype(jnp.bfloat16)
    local_keys = jnp.dot(tokens, w_key, preferred_element_type=jnp.float32).astype(jnp.bfloat16)
    local_values = jnp.dot(tokens, w_value, preferred_element_type=jnp.float32).astype(jnp.bfloat16)
    local_out = local_attention(queries, local_keys, local_values, kv_local, per_kv)
    own_flat = block_ids.reshape(-1)
    owner_of, local_of, rank_of, first_seen = plan_requests(own_flat, blocks_each)
    slot_of = owner_of * capacity + rank_of
    total_blocks = block_counts.shape[0]
    filled = jnp.sum(
        jnp.where(own_flat[:, None] == jnp.arange(total_blocks)[None, :], block_counts[None, :], 0),
        axis=1,
    )
    bias = jnp.where(jnp.arange(BLK)[None, :] < filled[:, None], 0.0, -jnp.inf)
    bias = bias.reshape(qblk_count, 1, topk_count * BLK).astype(jnp.float32)
    weights = memory_weights(slot_of, queries, bias, got_keys, kv_local, per_kv, topk_count)
    gate = jnp.repeat(jax.nn.sigmoid(gate_bias), HD).reshape(1, heads_local * HD)
    attn = mix_values(
        slot_of, weights, gate, local_out, got_values, kv_local, per_kv, topk_count
    )
    terms = jnp.dot(attn, w_out, preferred_element_type=jnp.float32)
    return lax.psum_scatter(terms.astype(jnp.bfloat16), "head", scatter_dimension=1, tiled=True)


def solution(mesh):
    in_specs = (
        P("mem", None),
        P(None, "head"),
        P(None, "head"),
        P(None, "head"),
        P("head", None),
        P("head"),
        P("mem", "head"),
        P("mem", "head"),
        P("mem", None),
        P(),
    )
    out_specs = P("mem", "head")
    return jax.shard_map(
        on_device, mesh=mesh, in_specs=in_specs, out_specs=out_specs, check_vma=False
    )
```

time: 1170 us -> 519 us (0.44)
  waiting for transfers between devices: 697 us -> 337 us
  local copies, waits for them, and re-layouts: 235 us -> 20.4 us
  Pallas kernels: 0 us -> 96.8 us
  matrix products: 125 us -> 37.4 us
  other arithmetic: 48.9 us -> 1.78 us
  blocking collectives: 32.5 us -> 0 us
    all_to_all x2, waiting for transfers between devices: 625 us -> 266 us  [the longest x1 173 us: on_device(): lax.all_to_all(key_blocks[send_slots], 'mem', split_axis=0, concat_axis=0...]
    dynamic_update_slice x8 -> x0, local copies, waits for them, and re-layouts: 121 us -> none  [on_device(): lax.map(memory_block, (queries.reshape(qblk_count, BLK, kv_local, per_kv,...]
    pallas_call x0 -> x4, Pallas kernels: none -> 96.8 us  [the longest x1 32.8 us: local_attention(): pl.pallas_call(functools.partial(local_kernel, per_kv), grid=(kv_local, r...]
    dot_general x17 -> x0, matrix products: 63.7 us -> none  [the longest x9 46.1 us: attend(): jnp.einsum('kgqs,skd->qkgd', weights, value_rows, preferred_element_type=...]
    sub x9 -> x0, other arithmetic: 47.5 us -> none  [the longest x8 46.9 us: attend(): weights = jnp.exp(scores - peak_score)]
    all_gather x1 -> x0, blocking collectives: 32.5 us -> none  [on_device(): lax.all_gather(block_ids, 'mem', axis=0, tiled=True)]
    gather x4 -> x2, local copies, waits for them, and re-layouts: 47.7 us -> 17.2 us  [the longest x1 8.63 us: on_device(): key_blocks[send_slots]]
    reshape x4 -> x1, local copies, waits for them, and re-layouts: 30.1 us -> 0.83 us  [on_device(): share_ids(block_ids, owners).reshape(owners, qblk_count * topk_count)]
  transfers between devices with their start and end apart: 3 -> 3, of which waited for: 3 -> 3; matrix products, arithmetic and copies ran while one was open for 8% -> 6% of each run, Pallas kernels for 0% -> 12%
where the time goes in v1:
time: 519 us; the launch traced here: 518 us
  waiting for transfers between devices  337 us (65%)
  Pallas kernels  96.8 us (19%)
  matrix products  37.4 us (7%)
  local copies, waits for them, and re-layouts  20.4 us (4%)
  between operations  13.6 us (3%)
  starting transfers between devices  10.5 us (2%)
    all_to_all x1, waiting for transfers between devices, on_device(): lax.all_to_all(key_blocks[send_slots], 'mem', split_axis=0, concat_axis=0...  173 us
    all_to_all x1, waiting for transfers between devices, on_device(): lax.all_to_all(value_blocks[send_slots], 'mem', split_axis=0, concat_axis...  92.9 us
    reduce_scatter x1, waiting for transfers between devices, on_device(): lax.psum_scatter(terms.astype(jnp.bfloat16), 'head', scatter_dimension=1,...  71.1 us
    pallas_call x1, Pallas kernels, local_attention(): pl.pallas_call(functools.partial(local_kernel, per_kv), grid=(kv_local, r...  32.8 us
    pallas_call x1, Pallas kernels, memory_weights(): pl.pallas_call(functools.partial(weights_kernel, per_kv, topk), grid_spec...  30.2 us
    pallas_call x1, Pallas kernels, mix_values(): pl.pallas_call(functools.partial(mix_kernel, per_kv, topk), grid_spec=plt...  24 us
    dot_general x1, matrix products, on_device(): terms = jnp.dot(attn, w_out, preferred_element_type=jnp.float32)  14.4 us
    dot_general x1, matrix products, on_device(): jnp.dot(tokens, w_query, preferred_element_type=jnp.float32)  11.4 us
  transfers between devices with their start and end apart: 3, of which 3 were waited for; matrix products, arithmetic and copies ran while one was open for 6% of the time, Pallas kernels for 12%

profile of v1, /device:TPU:0, one launch (start us, length us, event | category | flops | bytes accessed | tf_op | source)
XLA Modules:
  0.0 518.1 jit_solution(13510722317709061081)
XLA Ops:
  6.5 0.0 copy-start
  6.6 9.9 %share_ids.1 = s32[8,8,16]{2,1,0:T(8,128)} custom-call(s32[8,16]{1,0:T(8,128)} %ids_ref.1), custom_call_target="tpu_custom_call" | custom-call | tf_op jit(solution)/shard_map/share_ids/pallas_call | solution.py:44
  16.5 0.8 reshape.247
  17.3 0.4 and_reduce_fusion
  17.7 0.5 convert_reduce_fusion
  18.2 0.2 select_reduce_fusion.1
  18.4 0.1 reshape.253
  18.5 8.6 %gather_fusion = bf16[128,128,256]{2,1,0:T(8,128)(2,1)} fusion(bf16[64,128,256]{2,1,0:T(8,128)(2,1)} %bitcast.25, s32[1024]{0:T(1024)S(1)} %pad_clamp_fusion), kind=kCustom, calls=%fused_computation | custom fusion | bytes 16777728 | tf_op jit(solution)/shard_map/gather | solution.py:232
  27.2 5.4 %all-to-all-start = ((bf16[8,16,128,256]{3,2,1,0:T(8,128)(2,1)}), bf16[8,16,128,256]{3,2,1,0:T(8,128)(2,1)}, u32[]{:S(2)}, u32[]{:S(2)}) async-start(bf16[8,16,128,256]{3,2,1,0:T(8,128)(2,1)} %bitcast.24), calls=%async_computation | async-start | bytes 16777216 | tf_op jit(solution)/shard_map/all_to_all | solution.py:231
  32.6 8.6 %gather_fusion.1 = bf16[128,128,256]{2,1,0:T(8,128)(2,1)} fusion(bf16[64,128,256]{2,1,0:T(8,128)(2,1)} %bitcast.26, s32[1024]{0:T(1024)S(1)} %pad_clamp_fusion), kind=kCustom, calls=%fused_computation.1 | custom fusion | bytes 16777728 | tf_op jit(solution)/shard_map/gather | solution.py:235
  41.2 173.4 %all-to-all-done = bf16[8,16,128,256]{3,2,1,0:T(8,128)(2,1)} async-done(((bf16[8,16,128,256]{3,2,1,0:T(8,128)(2,1)}), bf16[8,16,128,256]{3,2,1,0:T(8,128)(2,1)}, u32[]{:S(2)}, u32[]{:S(2)}) %all-to-all-start) | async-done | bytes 8388640 | tf_op jit(solution)/shard_map/all_to_all | solution.py:231
  214.6 0.0 copy-start.3
  214.6 0.0 copy-start.4
  214.6 0.0 copy-start.6
  214.6 5.1 all-to-all-start.1
  219.7 0.0 reduce-scatter.2.cloned.1.call-start
  219.7 0.0 copy-done.3
  219.7 0.1 reshape.245
  219.8 0.2 and_reduce_fusion.1
  220.0 0.0 copy-done.4
  220.0 0.2 select_reduce_fusion
  220.2 0.1 lt.106
  220.3 0.0 copy-start.5
  220.3 0.2 convert_reduce_fusion.1
  220.5 0.0 copy-done.6
  220.5 0.0 copy-done
  220.5 0.0 slice-start
  220.6 5.9 %convolution_convert_fusion.2.v_ref = bf16[1024,256]{1,0:T(8,128)(2,1)S(1)} fusion(bf16[1024,4096]{1,0:T(8,128)(2,1)} %param.10, bf16[4096,256]{1,0:T(8,128)(2,1)S(1)} %copy-done), kind=kOutput, calls=%fused_computation.4 | convolution fusion | flops 2147745792 | bytes 11010048 | tf_op jit(solution)/shard_map/dot_general | solution.py:239
  226.4 0.0 copy-done.5
  226.4 0.0 slice-start.1
  226.4 5.9 %convolution_convert_fusion.3.k_ref = bf16[1024,256]{1,0:T(8,128)(2,1)S(1)} fusion(bf16[1024,4096]{1,0:T(8,128)(2,1)} %param.10, bf16[4096,256]{1,0:T(8,128)(2,1)S(1)} %copy-done.5), kind=kOutput, calls=%fused_computation.5 | convolution fusion | flops 2147745792 | bytes 11010048 | tf_op jit(solution)/shard_map/dot_general | solution.py:238
  232.3 0.0 slice-done
  232.3 0.0 slice-done.1
  232.3 11.4 %convolution_convert_fusion.1.q_ref = bf16[1024,1024]{1,0:T(8,128)(2,1)S(1)} fusion(bf16[1024,4096]{1,0:T(8,128)(2,1)S(1)} %bitcast.29, bf16[4096,1024]{1,0:T(8,128)(2,1)} %param.11), kind=kOutput, calls=%fused_computation.3 | convolution fusion | flops 8590983168 | bytes 18874368 | tf_op jit(solution)/shard_map/dot_general | solution.py:237
  243.7 32.8 %local_attention.1.local_ref = f32[1024,1024]{1,0:T(8,128)S(1)} custom-call(bf16[1024,1024]{1,0:T(8,128)(2,1)S(1)} %convolution_convert_fusion.1.q_ref, bf16[1024,256]{1,0:T(8,128)(2,1)S(1)} %convolution_convert_fusion.3.k_ref, bf16[1024,256]{1,0:T(8,128)(2,1)S(1)} %convolution_convert_fusion.2.v_ref), custom_call_target="tpu_custom_call" | custom-call | flops 4294967296 | bytes 6291456 | tf_op jit(solution)/shard_map/local_attention/pallas_call | solution.py:85
  276.5 0.0 copy-start.2
  276.5 1.9 copy-done.2
  278.4 0.1 lt.107
  278.5 0.1 compare_select_fusion.bias_ref
  278.6 30.2 %memory_weights.1.w_ref = bf16[2,8,4,128,2048]{4,3,2,1,0:T(8,128)(2,1)} custom-call(s32[128]{0:T(128)S(1)} %multiply_add_fusion.slot_ref, bf16[1024,1024]{1,0:T(8,128)(2,1)S(1)} %convolution_convert_fusion.1.q_ref, f32[8,1,2048]{2,1,0:T(1,128)S(1)} %compare_select_fusion.bias_ref, bf16[128,128,256]{2,1,0:T(8,128)(2,1)} %bitcast.5.k_ref), custom_call_target="tpu_custom_call" | custom-call | flops 4294967296 | bytes 33554432 | tf_op jit(solution)/shard_map/memory_weights/pallas_call | solution.py:126
  308.8 92.9 %all-to-all-done.1 = bf16[8,16,128,256]{3,2,1,0:T(8,128)(2,1)} async-done(((bf16[8,16,128,256]{3,2,1,0:T(8,128)(2,1)}), bf16[8,16,128,256]{3,2,1,0:T(8,128)(2,1)}, u32[]{:S(2)}, u32[]{:S(2)}) %all-to-all-start.1) | async-done | bytes 8388640 | tf_op jit(solution)/shard_map/all_to_all | solution.py:234
  401.7 0.1 broadcast_in_dim.20
  401.8 24.0 %mix_values.1 = bf16[1024,1024]{1,0:T(8,128)(2,1)S(1)} custom-call(s32[128]{0:T(128)S(1)} %multiply_add_fusion.slot_ref, bf16[2,8,4,128,2048]{4,3,2,1,0:T(8,128)(2,1)} %memory_weights.1.w_ref, f32[1,1024]{1,0:T(1,128)S(1)} %bitcast.22, f32[1024,1024]{1,0:T(8,128)} %copy-done.2, bf16[128,128,256]{2,1,0:T(8,128)(2,1)} %bitcast.9.v_ref), custom_call_target="tpu_custom_call" | custom-call | flops 4294967296 | bytes 33554432 | tf_op jit(solution)/shard_map/mix_values/pallas_call | solution.py:171
  425.7 0.0 copy-start.1
  425.7 14.4 %convolution_convert_fusion = bf16[1024,4096]{1,0:T(8,128)(2,1)} fusion(bf16[1024,1024]{1,0:T(8,128)(2,1)S(1)} %mix_values.1, bf16[1024,4096]{1,0:T(8,128)(2,1)} %param.14), kind=kOutput, calls=%fused_computation.2 | convolution fusion | flops 8594128896 | bytes 18874368 | tf_op jit(solution)/shard_map/dot_general | solution.py:256
  440.1 0.0 reduce-scatter.2.cloned.1.call-update
  440.1 71.1 %reduce-scatter.2.cloned.1.call-done = bf16[1024,1024]{1,0:T(8,128)(2,1)} async-done(((bf16[1024,4096]{1,0:T(8,128)(2,1)}), bf16[1024,1024]{1,0:T(8,128)(2,1)}) %reduce-scatter.2.cloned.1.call-update) | async-done | bytes 2097168 | tf_op jit(solution)/shard_map/reduce_scatter | solution.py:257
  511.2 0.0 copy-done.1
  (11 shorter events, 0.1 us)
Async XLA Ops:
  6.5 214.0 %copy-start = (bf16[4096,256]{1,0:T(8,128)(2,1)S(1)}, bf16[4096,256]{1,0:T(8,128)(2,1)}, u32[]{:S(2)}) copy-start(bf16[4096,256]{1,0:T(8,128)(2,1)} %param.13) | copy-start | bytes 6291460
  27.2 187.4 %all-to-all-start = ((bf16[8,16,128,256]{3,2,1,0:T(8,128)(2,1)}), bf16[8,16,128,256]{3,2,1,0:T(8,128)(2,1)}, u32[]{:S(2)}, u32[]{:S(2)}) async-start(bf16[8,16,128,256]{3,2,1,0:T(8,128)(2,1)} %bitcast.24), calls=%async_computation | async-start | bytes 16777216 | tf_op jit(solution)/shard_map/all_to_all | solution.py:231
  214.6 5.2 copy-start.3
  214.6 5.4 %copy-start.4 = (s32[512]{0:T(512)S(1)}, s32[512]{0:T(512)}, u32[]{:S(2)}) copy-start(s32[512]{0:T(512)} %param.19) | copy-start | bytes 6148
  214.6 5.9 %copy-start.6 = (f32[8]{0:T(128)S(1)}, f32[8]{0:T(128)}, u32[]{:S(2)}) copy-start(f32[8]{0:T(128)} %param.15) | copy-start | bytes 100
  214.6 187.1 %all-to-all-start.1 = ((bf16[8,16,128,256]{3,2,1,0:T(8,128)(2,1)}), bf16[8,16,128,256]{3,2,1,0:T(8,128)(2,1)}, u32[]{:S(2)}, u32[]{:S(2)}) async-start(bf16[8,16,128,256]{3,2,1,0:T(8,128)(2,1)} %bitcast.23), calls=%async_computation.1 | async-start | bytes 16777216 | tf_op jit(solution)/shard_map/all_to_all | solution.py:234
  219.7 291.5 %reduce-scatter.2.cloned.1.call-start = ((), (), s32[]{:S(2)}) async-start(), calls=%async_computation.3 | async-start | bytes 10485760 | tf_op jit(solution)/shard_map/reduce_scatter | solution.py:257
  220.3 6.1 %copy-start.5 = (bf16[4096,256]{1,0:T(8,128)(2,1)S(1)}, bf16[4096,256]{1,0:T(8,128)(2,1)}, u32[]{:S(2)}) copy-start(bf16[4096,256]{1,0:T(8,128)(2,1)} %param.12) | copy-start | bytes 6291460
  220.5 11.8 %slice-start = ((s8[8388608]{0:T(1024)(128)(4,1)}), s8[4194304]{0:T(1024)(128)(4,1)S(1)}, s32[]{:S(2)}) async-start(s8[8388608]{0:T(1024)(128)(4,1)} %bitcast.28), calls=%async_computation.4 | async-start | bytes 8388608
  226.4 5.9 %slice-start.1 = ((s8[8388608]{0:T(1024)(128)(4,1)}), s8[4194304]{0:T(1024)(128)(4,1)S(1)}, s32[]{:S(2)}) async-start(s8[8388608]{0:T(1024)(128)(4,1)} %bitcast.28), calls=%async_computation.5 | async-start | bytes 8388608
  276.5 1.9 copy-start.2
  425.7 85.5 %copy-start.1 = (bf16[4096,256]{1,0:T(8,128)(2,1)S(1)}, bf16[4096,256]{1,0:T(8,128)(2,1)}, u32[]{:S(2)}) copy-start(bf16[4096,256]{1,0:T(8,128)(2,1)} %param.13) | copy-start | bytes 6291460
Sparse Core Ops, SparseCore 0:
  440.3 70.9 reduce-scatter.1

commit v2 on v1

--- a/solution.py
+++ b/solution.py
@@ -11,48 +11,6 @@
 BLK = 128
 LOG2E = 1.4426950408889634
 MIB = 1 << 20
-
-
-def share_ids_kernel(owners, ids_ref, out_ref, send_sem, recv_sem):
-    me = lax.axis_index("mem")
-    barrier = pltpu.get_barrier_semaphore()
-    for step in range(1, owners):
-        peer = lax.rem(me + step, owners)
-        pl.semaphore_signal(
-            barrier, inc=1, device_id={"mem": peer}, device_id_type=pl.DeviceIdType.MESH
-        )
-    pl.semaphore_wait(barrier, owners - 1)
-    copies = []
-    for step in range(1, owners):
-        peer = lax.rem(me + step, owners)
-        copy = pltpu.make_async_remote_copy(
-            src_ref=ids_ref,
-            dst_ref=out_ref.at[me],
-            send_sem=send_sem.at[step],
-            recv_sem=recv_sem.at[step],
-            device_id={"mem": peer},
-            device_id_type=pl.DeviceIdType.MESH,
-        )
-        copy.start()
-        copies.append(copy)
-    out_ref[me] = ids_ref[...]
-    for copy in copies:
-        copy.wait()
-
-
-def share_ids(ids, owners):
-    return pl.pallas_call(
-        functools.partial(share_ids_kernel, owners),
-        out_shape=jax.ShapeDtypeStruct((owners,) + ids.shape, ids.dtype),
-        in_specs=[pl.BlockSpec(memory_space=pltpu.VMEM)],
-        out_specs=pl.BlockSpec(memory_space=pltpu.VMEM),
-        scratch_shapes=[
-            pltpu.SemaphoreType.DMA((owners,)),
-            pltpu.SemaphoreType.DMA((owners,)),
-        ],
-        compiler_params=pltpu.CompilerParams(collective_id=0, has_side_effects=True),
-        name="share_ids",
-    )(ids)
 
 
 def softmax_rows(scores):
@@ -149,8 +107,8 @@
     )(slots, queries, bias, keys)
 
 
-def mix_kernel(per_kv, topk, slot_ref, w_ref, gate_ref, local_ref, v_ref, out_ref, picked):
-    block = pl.program_id(1)
+def mix_kernel(per_kv, topk, first, slot_ref, w_ref, gate_ref, local_ref, v_ref, out_ref, picked):
+    block = pl.program_id(1) + first
     for pick in range(topk):
         picked[pick * BLK : (pick + 1) * BLK, :] = v_ref[slot_ref[block * topk + pick]]
     values = picked[...]
@@ -163,20 +121,21 @@
         )
 
 
-def mix_values(slots, weights, gate, local_out, values, kv_local, per_kv, topk):
-    rows, cols = local_out.shape
-    blocks = rows // BLK
+def mix_values(slots, weights, gate, local_out, values, kv_local, per_kv, topk, first, blocks):
+    rows, cols = blocks * BLK, local_out.shape[1]
     width = topk * BLK
     total = values.shape[0]
     return pl.pallas_call(
-        functools.partial(mix_kernel, per_kv, topk),
+        functools.partial(mix_kernel, per_kv, topk, first),
         grid_spec=pltpu.PrefetchScalarGridSpec(
             num_scalar_prefetch=1,
             grid=(kv_local, blocks),
             in_specs=[
-                pl.BlockSpec((1, 1, per_kv, BLK, width), lambda j, c, s: (j, c, 0, 0, 0)),
+                pl.BlockSpec(
+                    (1, 1, per_kv, BLK, width), lambda j, c, s: (j, c + first, 0, 0, 0)
+                ),
                 pl.BlockSpec((1, per_kv * HD), lambda j, c, s: (0, j)),
-                pl.BlockSpec((BLK, per_kv * HD), lambda j, c, s: (c, j)),
+                pl.BlockSpec((BLK, per_kv * HD), lambda j, c, s: (c + first, j)),
                 pl.BlockSpec((total, BLK, HD), lambda j, c, s: (0, 0, j)),
             ],
             out_specs=pl.BlockSpec((BLK, per_kv * HD), lambda j, c, s: (c, j)),
@@ -217,7 +176,13 @@
     blocks_each = mem_keys.shape[0] // BLK
     me_index = lax.axis_index("mem")
     capacity = max(2, topk_count * qblk_count // owners)
-    all_chosen = share_ids(block_ids, owners).reshape(owners, qblk_count * topk_count)
+    all_chosen = lax.all_to_all(
+        jnp.broadcast_to(block_ids.reshape(1, -1), (owners, qblk_count * topk_count)),
+        "mem",
+        split_axis=0,
+        concat_axis=0,
+        tiled=True,
+    )
 
     def send_list(flat_chosen):
         owner_of, local_of, rank_of, first_seen = plan_requests(flat_chosen, blocks_each)
@@ -250,11 +215,15 @@
     bias = bias.reshape(qblk_count, 1, topk_count * BLK).astype(jnp.float32)
     weights = memory_weights(slot_of, queries, bias, got_keys, kv_local, per_kv, topk_count)
     gate = jnp.repeat(jax.nn.sigmoid(gate_bias), HD).reshape(1, heads_local * HD)
-    attn = mix_values(
-        slot_of, weights, gate, local_out, got_values, kv_local, per_kv, topk_count
-    )
-    terms = jnp.dot(attn, w_out, preferred_element_type=jnp.float32)
-    return lax.psum_scatter(terms.astype(jnp.bfloat16), "head", scatter_dimension=1, tiled=True)
+    pieces = []
+    half = qblk_count // 2
+    for first, count in ((0, half), (half, qblk_count - half)):
+        attn = mix_values(
+            slot_of, weights, gate, local_out, got_values, kv_local, per_kv, topk_count, first, count
+        )
+        terms = jnp.dot(attn, w_out, preferred_element_type=jnp.float32).astype(jnp.bfloat16)
+        pieces.append(lax.psum_scatter(terms, "head", scatter_dimension=1, tiled=True))
+    return jnp.concatenate(pieces, axis=0)
 
 
 def solution(mesh):

time: 519 us -> 532 us (1.025)
  starting transfers between devices: 10.5 us -> 17.4 us
  Pallas kernels: 96.8 us -> 91.1 us
    all_to_all x0 -> x1, starting transfers between devices: none -> 7.25 us  [on_device(): lax.all_to_all(jnp.broadcast_to(block_ids.reshape(1, -1), (owners, qblk_c...]
    reduce_scatter x1 -> x2, waiting for transfers between devices: 71.1 us -> 63.9 us  [on_device(): lax.psum_scatter(terms, 'head', scatter_dimension=1, tiled=True)]
    all_to_all x0 -> x1, waiting for transfers between devices: none -> 6.37 us  [on_device(): lax.all_to_all(jnp.broadcast_to(block_ids.reshape(1, -1), (owners, qblk_c...]
    pallas_call x2, Pallas kernels: 33.9 us -> 28.2 us  [mix_values(): pl.pallas_call(functools.partial(mix_kernel, per_kv, topk, first), grid_s...]
    dot_general x1 -> x2, matrix products: 14.4 us -> 19.6 us  [on_device(): jnp.dot(attn, w_out, preferred_element_type=jnp.float32)]
  transfers between devices with their start and end apart: 3 -> 5, of which waited for: 3 -> 5; matrix products, arithmetic and copies ran while one was open for 6% -> 8% of each run, Pallas kernels for 12% -> 15%
where the time goes in v2:
time: 532 us
  waiting for transfers between devices  337 us (63%)
  Pallas kernels  91.1 us (17%)
  matrix products  42.6 us (8%)
  local copies, waits for them, and re-layouts  25.3 us (5%)
  starting transfers between devices  17.4 us (3%)
  between operations  13.7 us (3%)
    all_to_all x1, waiting for transfers between devices, on_device(): lax.all_to_all(key_blocks[send_slots], 'mem', split_axis=0, concat_axis=0...  173 us
    all_to_all x1, waiting for transfers between devices, on_device(): lax.all_to_all(value_blocks[send_slots], 'mem', split_axis=0, concat_axis...  93 us
    reduce_scatter x2, waiting for transfers between devices, on_device(): lax.psum_scatter(terms, 'head', scatter_dimension=1, tiled=True)  63.9 us
    pallas_call x1, Pallas kernels, local_attention(): pl.pallas_call(functools.partial(local_kernel, per_kv), grid=(kv_local, r...  32.7 us
    pallas_call x1, Pallas kernels, memory_weights(): pl.pallas_call(functools.partial(weights_kernel, per_kv, topk), grid_spec...  30.2 us
    pallas_call x2, Pallas kernels, mix_values(): pl.pallas_call(functools.partial(mix_kernel, per_kv, topk, first), grid_s...  28.2 us
    dot_general x2, matrix products, on_device(): jnp.dot(attn, w_out, preferred_element_type=jnp.float32)  19.6 us
    dot_general x1, matrix products, on_device(): jnp.dot(tokens, w_query, preferred_element_type=jnp.float32)  11.4 us
  transfers between devices with their start and end apart: 5, of which 5 were waited for; matrix products, arithmetic and copies ran while one was open for 8% of the time, Pallas kernels for 15%

profile of v2, /device:TPU:0, one launch (start us, length us, event | category | flops | bytes accessed | tf_op | source)
XLA Modules:
  0.0 531.6 jit_solution(2282302782238179365)
XLA Ops:
  6.5 0.0 copy-start
  6.5 0.9 reshape.196
  7.5 0.6 broadcast_in_dim.22
  8.1 7.3 %all-to-all-start = ((s32[8,1,128]{2,1,0:T(1,128)}), s32[8,1,128]{2,1,0:T(1,128)S(1)}, u32[]{:S(2)}, u32[]{:S(2)}) async-start(s32[8,1,128]{2,1,0:T(1,128)} %broadcast_in_dim.22), calls=%async_computation | async-start | bytes 8192 | tf_op jit(solution)/shard_map/all_to_all | solution.py:179
  15.3 6.4 %all-to-all-done = s32[8,1,128]{2,1,0:T(1,128)S(1)} async-done(((s32[8,1,128]{2,1,0:T(1,128)}), s32[8,1,128]{2,1,0:T(1,128)S(1)}, u32[]{:S(2)}, u32[]{:S(2)}) %all-to-all-start) | async-done | bytes 4128 | tf_op jit(solution)/shard_map/all_to_all | solution.py:179
  21.7 0.4 and_reduce_fusion
  22.1 0.5 convert_reduce_fusion
  22.6 0.2 select_reduce_fusion.1
  22.9 0.1 reshape.203
  23.0 8.6 %gather_fusion = bf16[128,128,256]{2,1,0:T(8,128)(2,1)} fusion(bf16[64,128,256]{2,1,0:T(8,128)(2,1)} %bitcast.43, s32[1024]{0:T(1024)S(1)} %pad_clamp_fusion), kind=kCustom, calls=%fused_computation | custom fusion | bytes 16777728 | tf_op jit(solution)/shard_map/gather | solution.py:197
  31.6 4.9 all-to-all-start.1
  36.5 8.6 %gather_fusion.1 = bf16[128,128,256]{2,1,0:T(8,128)(2,1)} fusion(bf16[64,128,256]{2,1,0:T(8,128)(2,1)} %bitcast.44, s32[1024]{0:T(1024)S(1)} %pad_clamp_fusion), kind=kCustom, calls=%fused_computation.1 | custom fusion | bytes 16777728 | tf_op jit(solution)/shard_map/gather | solution.py:200
  45.1 173.3 %all-to-all-done.1 = bf16[8,16,128,256]{3,2,1,0:T(8,128)(2,1)} async-done(((bf16[8,16,128,256]{3,2,1,0:T(8,128)(2,1)}), bf16[8,16,128,256]{3,2,1,0:T(8,128)(2,1)}, u32[]{:S(2)}, u32[]{:S(2)}) %all-to-all-start.1) | async-done | bytes 8388640 | tf_op jit(solution)/shard_map/all_to_all | solution.py:196
  218.4 0.0 copy-start.5
  218.4 0.0 copy-start.7
  218.4 5.1 all-to-all-start.2
  223.5 0.0 reduce-scatter.3.cloned.1.call-start
  223.6 0.2 and_reduce_fusion.1
  223.7 0.0 copy-done.5
  223.8 0.2 select_reduce_fusion
  223.9 0.1 lt.106
  224.0 0.0 copy-start.6
  224.0 0.2 convert_reduce_fusion.1
  224.2 0.0 copy-done.7
  224.3 0.0 copy-done
  224.3 0.0 slice-start
  224.3 5.9 %convolution_convert_fusion.3.v_ref = bf16[1024,256]{1,0:T(8,128)(2,1)S(1)} fusion(bf16[1024,4096]{1,0:T(8,128)(2,1)} %param.10, bf16[4096,256]{1,0:T(8,128)(2,1)S(1)} %copy-done), kind=kOutput, calls=%fused_computation.6 | convolution fusion | flops 2147745792 | bytes 11010048 | tf_op jit(solution)/shard_map/dot_general | solution.py:204
  230.1 0.0 copy-done.6
  230.2 0.0 slice-start.1
  230.2 5.9 %convolution_convert_fusion.4.k_ref = bf16[1024,256]{1,0:T(8,128)(2,1)S(1)} fusion(bf16[1024,4096]{1,0:T(8,128)(2,1)} %param.10, bf16[4096,256]{1,0:T(8,128)(2,1)S(1)} %copy-done.6), kind=kOutput, calls=%fused_computation.7 | convolution fusion | flops 2147745792 | bytes 11010048 | tf_op jit(solution)/shard_map/dot_general | solution.py:203
  236.0 0.0 slice-done
  236.0 0.0 slice-done.1
  236.1 11.4 %convolution_convert_fusion.2.q_ref = bf16[1024,1024]{1,0:T(8,128)(2,1)S(1)} fusion(bf16[1024,4096]{1,0:T(8,128)(2,1)S(1)} %bitcast.52, bf16[4096,1024]{1,0:T(8,128)(2,1)} %param.11), kind=kOutput, calls=%fused_computation.5 | convolution fusion | flops 8590983168 | bytes 18874368 | tf_op jit(solution)/shard_map/dot_general | solution.py:202
  247.4 32.7 %local_attention.1.local_ref = f32[1024,1024]{1,0:T(8,128)S(1)} custom-call(bf16[1024,1024]{1,0:T(8,128)(2,1)S(1)} %convolution_convert_fusion.2.q_ref, bf16[1024,256]{1,0:T(8,128)(2,1)S(1)} %convolution_convert_fusion.4.k_ref, bf16[1024,256]{1,0:T(8,128)(2,1)S(1)} %convolution_convert_fusion.3.v_ref), custom_call_target="tpu_custom_call" | custom-call | flops 4294967296 | bytes 6291456 | tf_op jit(solution)/shard_map/local_attention/pallas_call | solution.py:43
  280.2 0.0 copy-start.2
  280.2 1.9 copy-done.2
  282.1 0.1 lt.107
  282.2 0.1 compare_select_fusion.bias_ref
  282.3 30.2 %memory_weights.1.w_ref = bf16[2,8,4,128,2048]{4,3,2,1,0:T(8,128)(2,1)} custom-call(s32[128]{0:T(128)S(1)} %multiply_add_fusion.slot_ref, bf16[1024,1024]{1,0:T(8,128)(2,1)S(1)} %convolution_convert_fusion.2.q_ref, f32[8,1,2048]{2,1,0:T(1,128)S(1)} %compare_select_fusion.bias_ref, bf16[128,128,256]{2,1,0:T(8,128)(2,1)} %bitcast.14.k_ref), custom_call_target="tpu_custom_call" | custom-call | flops 4294967296 | bytes 33554432 | tf_op jit(solution)/shard_map/memory_weights/pallas_call | solution.py:84
  312.5 93.0 %all-to-all-done.2 = bf16[8,16,128,256]{3,2,1,0:T(8,128)(2,1)} async-done(((bf16[8,16,128,256]{3,2,1,0:T(8,128)(2,1)}), bf16[8,16,128,256]{3,2,1,0:T(8,128)(2,1)}, u32[]{:S(2)}, u32[]{:S(2)}) %all-to-all-start.2) | async-done | bytes 8388640 | tf_op jit(solution)/shard_map/all_to_all | solution.py:199
  405.5 0.1 broadcast_in_dim.23
  405.6 0.0 copy-start.3
  405.6 2.2 copy-done.3
  407.8 13.4 %mix_values.2 = bf16[512,1024]{1,0:T(8,128)(2,1)S(1)} custom-call(s32[128]{0:T(128)S(1)} %multiply_add_fusion.slot_ref, bf16[2,8,4,128,2048]{4,3,2,1,0:T(8,128)(2,1)} %memory_weights.1.w_ref, f32[1,1024]{1,0:T(1,128)S(1)} %bitcast.39, f32[1024,1024]{1,0:T(8,128)S(1)} %copy-done.3, bf16[128,128,256]{2,1,0:T(8,128)(2,1)} %bitcast.18.v_ref), custom_call_target="tpu_custom_call" | custom-call | flops 2147483648 | bytes 16777216 | tf_op jit(solution)/shard_map/mix_values/pallas_call | solution.py:128
  421.2 9.4 %convolution_convert_fusion.1 = bf16[512,4096]{1,0:T(8,128)(2,1)} fusion(bf16[512,1024]{1,0:T(8,128)(2,1)S(1)} %mix_values.2, bf16[1024,4096]{1,0:T(8,128)(2,1)} %param.14), kind=kOutput, calls=%fused_computation.3 | convolution fusion | flops 4297064448 | bytes 13631488 | tf_op jit(solution)/shard_map/dot_general | solution.py:224
  430.6 0.0 reduce-scatter.3.cloned.1.call-update
  430.6 0.0 reduce-scatter.5.cloned.1.call-start
  430.6 0.0 copy-start.4
  430.6 2.2 copy-done.4
  432.8 14.8 %mix_values.3 = bf16[512,1024]{1,0:T(8,128)(2,1)S(1)} custom-call(s32[128]{0:T(128)S(1)} %multiply_add_fusion.slot_ref, bf16[2,8,4,128,2048]{4,3,2,1,0:T(8,128)(2,1)} %memory_weights.1.w_ref, f32[1,1024]{1,0:T(1,128)S(1)} %bitcast.40, f32[1024,1024]{1,0:T(8,128)S(1)} %copy-done.4, bf16[128,128,256]{2,1,0:T(8,128)(2,1)} %bitcast.18.v_ref), custom_call_target="tpu_custom_call" | custom-call | flops 2147483648 | bytes 16777216 | tf_op jit(solution)/shard_map/mix_values/pallas_call | solution.py:128
  447.6 0.0 copy-start.1
  447.6 10.2 %convolution_convert_fusion = bf16[512,4096]{1,0:T(8,128)(2,1)} fusion(bf16[512,1024]{1,0:T(8,128)(2,1)S(1)} %mix_values.3, bf16[1024,4096]{1,0:T(8,128)(2,1)} %param.14), kind=kOutput, calls=%fused_computation.2 | convolution fusion | flops 4297064448 | bytes 13631488 | tf_op jit(solution)/shard_map/dot_general | solution.py:224
  457.8 0.0 reduce-scatter.5.cloned.1.call-update
  457.8 16.7 %reduce-scatter.3.cloned.1.call-done = bf16[512,1024]{1,0:T(8,128)(2,1)} async-done(((bf16[512,4096]{1,0:T(8,128)(2,1)}), bf16[512,1024]{1,0:T(8,128)(2,1)}) %reduce-scatter.3.cloned.1.call-update) | async-done | bytes 1048592 | tf_op jit(solution)/shard_map/reduce_scatter | solution.py:225
  474.5 47.2 %reduce-scatter.5.cloned.1.call-done = bf16[512,1024]{1,0:T(8,128)(2,1)} async-done(((bf16[512,4096]{1,0:T(8,128)(2,1)}), bf16[512,1024]{1,0:T(8,128)(2,1)}) %reduce-scatter.5.cloned.1.call-update) | async-done | bytes 1048592 | tf_op jit(solution)/shard_map/reduce_scatter | solution.py:225
  521.7 3.0 pad_maximum_fusion
  524.8 0.0 copy-done.1
  (13 shorter events, 0.1 us)
Async XLA Ops:
  6.5 217.7 %copy-start = (bf16[4096,256]{1,0:T(8,128)(2,1)S(1)}, bf16[4096,256]{1,0:T(8,128)(2,1)}, u32[]{:S(2)}) copy-start(bf16[4096,256]{1,0:T(8,128)(2,1)} %param.13) | copy-start | bytes 6291460
  8.1 13.6 %all-to-all-start = ((s32[8,1,128]{2,1,0:T(1,128)}), s32[8,1,128]{2,1,0:T(1,128)S(1)}, u32[]{:S(2)}, u32[]{:S(2)}) async-start(s32[8,1,128]{2,1,0:T(1,128)} %broadcast_in_dim.22), calls=%async_computation | async-start | bytes 8192 | tf_op jit(solution)/shard_map/all_to_all | solution.py:179
  31.6 186.8 %all-to-all-start.1 = ((bf16[8,16,128,256]{3,2,1,0:T(8,128)(2,1)}), bf16[8,16,128,256]{3,2,1,0:T(8,128)(2,1)}, u32[]{:S(2)}, u32[]{:S(2)}) async-start(bf16[8,16,128,256]{3,2,1,0:T(8,128)(2,1)} %bitcast.42), calls=%async_computation.1 | async-start | bytes 16777216 | tf_op jit(solution)/shard_map/all_to_all | solution.py:196
  218.4 5.3 %copy-start.5 = (s32[512]{0:T(512)S(1)}, s32[512]{0:T(512)}, u32[]{:S(2)}) copy-start(s32[512]{0:T(512)} %param.19) | copy-start | bytes 6148
  218.4 5.8 %copy-start.7 = (f32[8]{0:T(128)S(1)}, f32[8]{0:T(128)}, u32[]{:S(2)}) copy-start(f32[8]{0:T(128)} %param.15) | copy-start | bytes 100
  218.4 187.1 %all-to-all-start.2 = ((bf16[8,16,128,256]{3,2,1,0:T(8,128)(2,1)}), bf16[8,16,128,256]{3,2,1,0:T(8,128)(2,1)}, u32[]{:S(2)}, u32[]{:S(2)}) async-start(bf16[8,16,128,256]{3,2,1,0:T(8,128)(2,1)} %bitcast.41), calls=%async_computation.2 | async-start | bytes 16777216 | tf_op jit(solution)/shard_map/all_to_all | solution.py:199
  223.5 251.0 %reduce-scatter.3.cloned.1.call-start = ((), (), s32[]{:S(2)}) async-start(), calls=%async_computation.5 | async-start | bytes 5242880 | tf_op jit(solution)/shard_map/reduce_scatter | solution.py:225
  224.0 6.1 %copy-start.6 = (bf16[4096,256]{1,0:T(8,128)(2,1)S(1)}, bf16[4096,256]{1,0:T(8,128)(2,1)}, u32[]{:S(2)}) copy-start(bf16[4096,256]{1,0:T(8,128)(2,1)} %param.12) | copy-start | bytes 6291460
  224.3 11.8 %slice-start = ((s8[8388608]{0:T(1024)(128)(4,1)}), s8[4194304]{0:T(1024)(128)(4,1)S(1)}, s32[]{:S(2)}) async-start(s8[8388608]{0:T(1024)(128)(4,1)} %bitcast.51), calls=%async_computation.7 | async-start | bytes 8388608
  230.2 5.9 %slice-start.1 = ((s8[8388608]{0:T(1024)(128)(4,1)}), s8[4194304]{0:T(1024)(128)(4,1)S(1)}, s32[]{:S(2)}) async-start(s8[8388608]{0:T(1024)(128)(4,1)} %bitcast.51), calls=%async_computation.8 | async-start | bytes 8388608
  280.2 1.9 copy-start.2
  405.6 2.2 copy-start.3
  430.6 91.1 %reduce-scatter.5.cloned.1.call-start = ((), (), s32[]{:S(2)}) async-start(), calls=%async_computation.6 | async-start | bytes 5242880 | tf_op jit(solution)/shard_map/reduce_scatter | solution.py:225
  430.6 2.2 copy-start.4
  447.6 77.1 %copy-start.1 = (bf16[4096,256]{1,0:T(8,128)(2,1)S(1)}, bf16[4096,256]{1,0:T(8,128)(2,1)}, u32[]{:S(2)}) copy-start(bf16[4096,256]{1,0:T(8,128)(2,1)} %param.13) | copy-start | bytes 6291460
Sparse Core Ops, SparseCore 0:
  430.7 43.7 reduce-scatter.2
  477.2 44.5 reduce-scatter.4
